TPU v7x, 128 devices: a whole 4x4x4 slice. The times are simulated.
128 devices in a mesh: gx: 16 (over y_hi, x, core), gy: 8 (over y_lo, z).
Axes of the slice: x: 4, y: 4 (y_hi: 2, y_lo: 2; y = y_hi * 2 + y_lo), z: 4, core: 2. Of those that a mesh axis runs over, the one named last changes fastest.
Arguments:
- res_charge: float32 [262144], P(('gx', 'gy')), may hold values from -6 to 6
- res_frac: float32 [3, 262144], P(None, ('gx', 'gy')), may hold values from 0 to 1
- res_cell: int32 [262144], P(('gx', 'gy')), may hold values from 0 to 65535
- res_count: int32 [128], P(('gx', 'gy')), may hold values from 1024 to 2048, as said below
- mov_charge: float32 [65536], P(('gx', 'gy')), may hold values from -6 to 6
- mov_frac: float32 [3, 65536], P(None, ('gx', 'gy')), may hold values from 0 to 1
- mov_cell: int32 [65536], P(('gx', 'gy')), may hold values from 0 to 65535
- mov_dest: int32 [65536, 1], P(('gx', 'gy')), may hold values from 0 to 127; in each aligned block of 512 rows (0 to 511, 512 to 1023, ...) at most 8 rows name the same one
- fine_taps: float32 [3, 13], replicated, may hold values from -3 to 3
- coarse_taps: float32 [3, 13], replicated, may hold values from -3 to 3
Outputs:
- res_potential: float32 [262144], P(('gx', 'gy'))
- arrived_potential: float32 [128, 1024], P(('gx', 'gy'))
- grid_potential: float32 [512, 128, 128], P('gx', 'gy')
Inputs may be any that keep to these rules, and one draw needn't show every extreme that they name: `res_count`: a multiple of 128; some box has exactly 2048 live atoms. `mov_dest`: among the rows of one source box, at most 8 name the same destination, a bound that some block reaches of them.
All inputs are finite; a program needn't handle non-finite values.
Results may differ from a plain program's by a relative error of at most 0.0048.
Values sent between devices are 32-bit elements; how exact they have to be, the bound alone decides.
A program may use at most 64 MiB of HBM per device.

v0:
```python
import jax
import jax.numpy as jnp
from jax import lax
from jax.sharding import PartitionSpec as P

CX = 32
CY = 16
NZ = 128


def from_behind(value, axis, steps):
    count = lax.axis_size(axis)
    pairs = [(source, (source + steps) % count) for source in range(count)]
    return lax.ppermute(value, axis, pairs)


def padded_2(x, sides, width):
    for axis, dim in sides:
        size, length = (lax.axis_size(axis), x.shape[dim])
        up = [(i, (i + 1) % size) for i in range(size)]
        down = [(j, i) for i, j in up]
        last = lax.slice_in_dim(x, length - width, length, axis=dim)
        initial = lax.slice_in_dim(x, 0, width, axis=dim)
        before = lax.ppermute(last, axis, up)
        after = lax.ppermute(initial, axis, down)
        x = jnp.concatenate([before, x, after], axis=dim)
    return x


def spline_weights(fracs):
    rest = 1.0 - fracs
    cube = fracs * fracs * fracs
    square = fracs * fracs
    return jnp.stack(
        [
            rest * rest * rest / 6.0,
            (3.0 * cube - 6.0 * square + 4.0) / 6.0,
            (-3.0 * cube + 3.0 * square + 3.0 * fracs + 1.0) / 6.0,
            cube / 6.0,
        ]
    )


def stencil(first, weights, length, wrapped):
    columns = jnp.arange(length, dtype=jnp.int32)[None, :]
    result = jnp.zeros((first.shape[0], length), jnp.float32)
    for offset_k in range(4):
        where_at = first + offset_k
        if wrapped:
            where_at = where_at % length
        result = result + jnp.where(columns == where_at[:, None], weights[offset_k][:, None], 0.0)
    return result


def factors(fracs, cells):
    cell_x = cells // (CY * NZ)
    cell_y = cells // NZ % CY
    cell_z = cells % NZ
    x_weights = stencil(cell_x, spline_weights(fracs[0]), CX + 3, False)
    y_weights = stencil(cell_y, spline_weights(fracs[1]), CY + 3, False)
    z_weights = stencil(cell_z, spline_weights(fracs[2]), NZ, True)
    yz_weights = (y_weights[:, :, None] * z_weights[:, None, :]).astype(jnp.bfloat16)
    return (x_weights, yz_weights.reshape(cells.shape[0], (CY + 3) * NZ))


def blocked(charges, fracs, cells):
    rows = charges.shape[0]
    block_rows = min(512, rows)
    blocks = rows // block_rows
    return (
        charges.reshape(blocks, block_rows),
        fracs.reshape(3, blocks, block_rows).transpose(1, 0, 2),
        cells.reshape(blocks, block_rows),
    )


def spread(charges, fracs, cells):

    def advance(running, pieces):
        block_charge, block_frac, block_cell = pieces
        x_weights, yz_weights = factors(block_frac, block_cell)
        x_charge = (x_weights * block_charge[:, None]).astype(jnp.bfloat16)
        added = lax.dot_general(
            x_charge, yz_weights, (((0,), (0,)), ((), ())), preferred_element_type=jnp.float32
        )
        return (running + added, None)

    start_grid = jnp.zeros((CX + 3, (CY + 3) * NZ), jnp.float32)
    running, _ = lax.scan(advance, start_grid, blocked(charges, fracs, cells))
    return running


def sample(half_grid, charges, fracs, cells):

    def evaluate(pieces):
        block_charge, block_frac, block_cell = pieces
        x_weights, yz_weights = factors(block_frac, block_cell)
        partial_value = lax.dot_general(
            half_grid, yz_weights, (((1,), (1,)), ((), ())), preferred_element_type=jnp.float32
        )
        x_plain = lax.optimization_barrier(x_weights.astype(jnp.bfloat16)).astype(jnp.float32)
        return jnp.sum(x_plain.T * partial_value, axis=0)

    return lax.map(evaluate, blocked(charges, fracs, cells)).reshape(-1)


def along(field, filter_taps, along_dim, offset, length):
    summed = jnp.zeros(
        field.shape[:along_dim] + (length,) + field.shape[along_dim + 1 :], jnp.float32
    )
    for tap_index in range(filter_taps.shape[0]):
        summed = summed + filter_taps[tap_index] * lax.slice_in_dim(
            field, offset + tap_index, offset + tap_index + length, axis=along_dim
        )
    return summed


def beside_all(field, filter_taps):
    summed = jnp.zeros_like(field)
    half_width = filter_taps.shape[0] // 2
    for tap_index in range(filter_taps.shape[0]):
        summed = summed + filter_taps[tap_index] * jnp.roll(field, half_width - tap_index, axis=2)
    return summed


def level_field(padded, filter_taps, margin, length_x, length_y):
    half_width = filter_taps.shape[1] // 2
    field = along(padded, filter_taps[0], 0, margin - half_width, length_x)
    field = along(field, filter_taps[1], 1, margin - half_width, length_y)
    return beside_all(field, filter_taps[2])


def coarsen(field):
    size_a, size_b, size_c = field.shape
    return field.reshape(size_a // 2, 2, size_b // 2, 2, size_c // 2, 2).sum(axis=(1, 3, 5))


def on_device(
    res_charge,
    res_frac,
    res_cell,
    res_count,
    mov_charge,
    mov_frac,
    mov_cell,
    mov_dest,
    fine_taps,
    coarse_taps,
):
    count_gx = lax.axis_size("gx")
    count_gy = lax.axis_size("gy")
    devices = count_gx * count_gy
    moving = mov_charge.shape[0]
    slots = 2 * moving // devices
    targets = mov_dest[:, 0]
    hits = (targets[:, None] == jnp.arange(devices, dtype=jnp.int32)[None, :]).astype(jnp.float32)
    positions = jnp.arange(moving, dtype=jnp.int32)
    lower = (positions[:, None] >= positions[None, :]).astype(jnp.float32)
    ranks = jnp.dot(lower, hits, precision=lax.Precision.HIGHEST)
    slot = (jnp.sum(hits * ranks, axis=1) - 1.0).astype(jnp.int32)
    target_slot = targets * slots + slot
    placing = (
        target_slot[:, None] == jnp.arange(devices * slots, dtype=jnp.int32)[None, :]
    ).astype(jnp.float32)
    payload = jnp.concatenate(
        [mov_charge[None, :], mov_frac, (mov_cell.astype(jnp.float32) + 1.0)[None, :]], 0
    )
    packed = jnp.dot(payload, placing, precision=lax.Precision.HIGHEST)
    arrived = lax.all_to_all(
        packed.reshape(5, devices, slots), ("gx", "gy"), split_axis=1, concat_axis=1, tiled=True
    )
    arrived = arrived.reshape(5, devices * slots)
    live = jnp.arange(res_charge.shape[0], dtype=jnp.int32) < res_count[0]
    live_charge = jnp.where(live, res_charge, 0.0)
    resident_grid = spread(live_charge, res_frac, res_cell)
    occupied = arrived[4] > 0.5
    arrived_cell = jnp.maximum(arrived[4] - 1.0, 0.0).astype(jnp.int32)
    arrived_grid = spread(arrived[0], arrived[1:4], arrived_cell)
    extended = (resident_grid + arrived_grid).reshape(CX + 3, CY + 3, NZ)
    upper_x = from_behind(extended[CX:], "gx", 1)
    extended = extended[:CX].at[:3].add(upper_x)
    upper_y = from_behind(extended[:, CY:], "gy", 1)
    charge_grid = extended[:, :CY].at[:, :3].add(upper_y)
    fine_padded = padded_2(charge_grid, (("gx", 0), ("gy", 1)), 9)
    coarse_padded = padded_2(coarsen(charge_grid), (("gx", 0), ("gy", 1)), 8)
    fine_field = level_field(fine_padded, fine_taps, 9, CX + 3, CY + 3)
    coarse_field = level_field(coarse_padded, coarse_taps, 8, CX // 2 + 2, CY // 2 + 2)
    spread_coarse = jnp.repeat(jnp.repeat(jnp.repeat(coarse_field, 2, 0), 2, 1), 2, 2)[
        : CX + 3, : CY + 3
    ]
    field_ext = fine_field + spread_coarse
    grid_potential = field_ext[:CX, :CY]
    half_grid = field_ext.astype(jnp.bfloat16).reshape(CX + 3, (CY + 3) * NZ)
    resident_values = sample(half_grid, live_charge, res_frac, res_cell)
    arrived_values = sample(half_grid, arrived[0], arrived[1:4], arrived_cell)
    res_potential = jnp.where(live, resident_values, 0.0)
    arrived_potential = jnp.where(occupied, arrived_values, 0.0)[None, :]
    return (res_potential, arrived_potential, grid_potential)


def solution(mesh):
    return jax.shard_map(
        on_device,
        mesh=mesh,
        in_specs=(
            P(("gx", "gy")),
            P(None, ("gx", "gy")),
            P(("gx", "gy")),
            P(("gx", "gy")),
            P(("gx", "gy")),
            P(None, ("gx", "gy")),
            P(("gx", "gy")),
            P(("gx", "gy"), None),
            P(),
            P(),
        ),
        out_specs=(P(("gx", "gy")), P(("gx", "gy"), None), P("gx", "gy", None)),
        check_vma=False,
    )
```

profile of v0, /device:TPU:0, one launch (start us, length us, event | category | flops | bytes accessed | tf_op | source)
XLA Modules:
  0.0 182.6 jit_solution(335659025685137201)
XLA Ops:
  3.1 1.5 fusion.156
  5.9 11.7 %all-to-all-start = ((f32[5,128,8]{2,0,1:T(8,128)}), f32[5,128,8]{2,0,1:T(8,128)}, u32[]{:S(2)}, u32[]{:S(2)}) async-start(f32[5,128,8]{2,0,1:T(8,128)} %copy.17), calls=%async_computation | async-start | bytes 1048576 | tf_op jit(solution)/shard_map/all_to_all | solution.py:169
  19.8 9.6 %while.58 = (s32[]{:T(128)}, f32[35,2432]{1,0:T(8,128)S(1)}, s32[4,512]{1,0:T(4,128)S(1)}, f32[4,3,512]{2,1,0:T(4,128)S(1)}, f32[4,512]{1,0:T(4,128)S(1)}, /*index=5*/s32[]{:T(128)}, s32[]{:T(128)}, s32[]{}, s32[]{}) while((s32[]{:T(128)}, f32[35,2432]{1,0:T(8,128)S(1)}, s32[4,512]{1,0:T(4,128)S(1)}, f32[4,3,512]{2,1,0:T(4,128)S(1)}, ...), condition=%wide.region_1.2_spmd.clone, body=%wide.region_0.0_spmd.clone.sunk | while | flops 90961152 | bytes 6397083 | solution.py:89
  20.7 1.5 convolution_add_fusion.4
  23.1 1.5 convolution_add_fusion.4
  25.5 1.5 convolution_add_fusion.4
  27.9 1.5 convolution_add_fusion.4
  30.8 1.3 convert_reduce_fusion
  32.2 1.1 slice.1151
  33.5 1.2 slice_reduce_fusion
  34.8 4.8 %while.59 = (s32[]{:T(128)}, f32[35,2432]{1,0:T(8,128)S(1)}, s32[2,512]{1,0:T(2,128)S(1)}, f32[2,3,512]{2,1,0:T(4,128)S(1)}, f32[2,512]{1,0:T(2,128)S(1)}, /*index=5*/s32[]{:T(128)}, s32[]{:T(128)}, s32[]{}, s32[]{}) while((s32[]{:T(128)}, f32[35,2432]{1,0:T(8,128)S(1)}, s32[2,512]{1,0:T(2,128)S(1)}, f32[2,3,512]{2,1,0:T(4,128)S(1)}, ...), condition=%wide.region_4.5_spmd.clone, body=%wide.region_3.4_spmd.clone.sunk | while | flops 90961152 | bytes 6397083 | solution.py:89
  35.7 1.5 convolution_add_fusion.5
  38.1 1.5 convolution_add_fusion.5
  41.8 4.9 %collective-permute-done = f32[3,19,128]{2,1,0:T(8,128)S(1)} collective-permute-done((f32[3,19,128]{2,1,0:T(8,128)S(1)}, f32[3,19,128]{2,1,0:T(8,128)S(1)}, u32[]{:S(2)}, u32[]{:S(2)}) %collective-permute-start) | collective-permute-done | bytes 29216 | tf_op jit(solution)/shard_map/ppermute | solution.py:14
  47.2 1.3 compare_reduce_fusion
  48.6 4.6 %collective-permute-done.1 = f32[32,3,128]{2,1,0:T(4,128)S(1)} collective-permute-done((f32[32,3,128]{2,1,0:T(4,128)S(1)}, f32[32,3,128]{2,1,0:T(4,128)S(1)}, u32[]{:S(2)}, u32[]{:S(2)}) %collective-permute-start.1) | collective-permute-done | bytes 49184 | tf_op jit(solution)/shard_map/ppermute | solution.py:14
  53.5 18.1 %reshape.3264 = f32[16,2,8,2,64,2]{5,4,3,2,1,0:T(8,128)} reshape(f32[32,16,128]{2,1,0:T(8,128)S(1)} %scatter-add.9) | data formatting | bytes 524288 | tf_op jit(solution)/shard_map/reshape | solution.py:135
  71.6 7.0 %reduce_sum.45 = f32[16,8,64]{2,1,0:T(8,128)S(1)} reduce(f32[16,2,8,2,64,2]{5,4,3,2,1,0:T(8,128)} %reshape.3264, f32[]{:T(128)} %constant.878.clone.1), dimensions={1,3,5}, to_apply=%region_5.6 | reduce | flops 57344 | bytes 294916 | tf_op jit(solution)/shard_map/reduce_sum | solution.py:135
  79.2 5.0 %collective-permute-start.3 = (f32[9,16,128]{2,1,0:T(8,128)S(1)}, f32[9,16,128]{2,1,0:T(8,128)S(1)}, u32[]{:S(2)}, u32[]{:S(2)}) collective-permute-start(f32[9,16,128]{2,1,0:T(8,128)S(1)} %get-tuple-element.678), channel_id=1, source_target_pairs={{8,0},{16,8},{24,16},{32,24},{40,32},{48,40},{56,48},{64,56},{72,6... | collective-permute-start | bytes 221192 | tf_op jit(solution)/shard_map/ppermute | solution.py:25
  84.2 1.5 collective-permute-done.6
  87.9 3.8 %collective-permute-done.2 = f32[9,16,128]{2,1,0:T(8,128)S(1)} collective-permute-done((f32[9,16,128]{2,1,0:T(8,128)S(1)}, f32[9,16,128]{2,1,0:T(8,128)S(1)}, u32[]{:S(2)}, u32[]{:S(2)}) %collective-permute-start.2) | collective-permute-done | bytes 73760 | tf_op jit(solution)/shard_map/ppermute | solution.py:24
  92.7 1.2 collective-permute-start.4
  93.9 1.4 collective-permute-done.8
  95.3 8.3 %fusion.196 = f32[18,24,64]{2,1,0:T(8,128)S(1)} fusion(f32[32,24,64]{2,1,0:T(8,128)S(1)} %pad_maximum_fusion.2, f32[]{:T(128)} %bitcast.75, f32[]{:T(128)} %bitcast.74, f32[]{:T(128)} %bitcast.73, f32[]{:T(128)} %bitcast.72, f32[]{:T(128)} %bitcast.71, f32[]{:T(128)} %bitcast.70, f32[]{:T(128)} %bitcast.69, f32[]{:T(128)} %bitcast.68, f32[]{:T(128)} %bitcast.67, ...), kind=kLoop, calls=%fused_computation.501 | loop fusion | flops 691200 | bytes 1548340 | tf_op jit(solution)/shard_map/add | solution.py:112
  103.6 8.3 %fusion.208 = f32[18,10,64]{2,1,0:T(8,128)S(1)} fusion(f32[18,24,64]{2,1,0:T(8,128)S(1)} %fusion.196, f32[]{:T(128)} %bitcast.87, f32[]{:T(128)} %bitcast.86, f32[]{:T(128)} %bitcast.85, f32[]{:T(128)} %bitcast.84, f32[]{:T(128)} %bitcast.83, f32[]{:T(128)} %bitcast.82, f32[]{:T(128)} %bitcast.81, f32[]{:T(128)} %bitcast.80, f32[]{:T(128)} %bitcast.79, ...), kind=kLoop, calls=%fused_computation.526 | loop fusion | flops 288000 | bytes 645172 | tf_op jit(solution)/shard_map/add | solution.py:112
  113.2 17.0 %fusion.231 = f32[18,10,64]{2,1,0:T(8,128)S(1)} fusion(f32[18,10,58]{2,1,0:T(8,128)S(1)} %get-tuple-element.680, f32[18,10,6]{2,1,0:T(8,128)S(1)} %get-tuple-element.682, f32[18,10,59]{2,1,0:T(8,128)S(1)} %get-tuple-element.684, f32[18,10,5]{2,1,0:T(8,128)S(1)} %get-tuple-element.686, f32[18,10,60]{2,1,0:T(8,128)S(1)} %get-tuple-element.688, ...), kind=kLoop, calls=%fused_computation.562 | loop fusion | flops 714240 | bytes 1198184 | tf_op jit(solution)/shard_map/add | solution.py:122
  131.9 1.1 pad_maximum_fusion
  133.0 8.8 %fusion.159 = f32[35,34,128]{2,1,0:T(8,128)S(1)} fusion(f32[50,34,128]{2,1,0:T(8,128)S(1)} %pad_maximum_fusion, f32[]{:T(128)} %bitcast.36, f32[]{:T(128)} %bitcast.35, f32[]{:T(128)} %bitcast.34, f32[]{:T(128)} %bitcast.33, f32[]{:T(128)} %bitcast.32, f32[]{:T(128)} %bitcast.31, f32[]{:T(128)} %bitcast.30, f32[]{:T(128)} %bitcast.29, f32[]{:T(128)} %bitcast.28, ...), kind=kLoop, calls=%fused_computation.422 | loop fusion | flops 3808000 | bytes 8529972 | tf_op jit(solution)/shard_map/add | solution.py:112
  141.7 8.7 %fusion.171 = f32[35,19,128]{2,1,0:T(8,128)S(1)} fusion(f32[35,34,128]{2,1,0:T(8,128)S(1)} %fusion.159, f32[]{:T(128)} %bitcast.48, f32[]{:T(128)} %bitcast.47, f32[]{:T(128)} %bitcast.46, f32[]{:T(128)} %bitcast.45, f32[]{:T(128)} %bitcast.44, f32[]{:T(128)} %bitcast.43, f32[]{:T(128)} %bitcast.42, f32[]{:T(128)} %bitcast.41, f32[]{:T(128)} %bitcast.40, ...), kind=kLoop, calls=%fused_computation.447 | loop fusion | flops 2128000 | bytes 4766772 | tf_op jit(solution)/shard_map/add | solution.py:112
  152.8 18.6 %fusion.241 = (bf16[35,19,128]{2,1,0:T(8,128)(2,1)S(1)}, f32[35,19,128]{2,1,0:T(8,128)S(1)}) fusion(f32[35,19,128]{2,1,0:T(8,128)S(1)} %copy.24, f32[35,19,6]{2,1,0:T(8,128)S(1)} %get-tuple-element.650, f32[35,19,122]{2,1,0:T(8,128)S(1)} %get-tuple-element.652, f32[]{:T(128)} %bitcast.60, f32[35,19,5]{2,1,0:T(8,128)S(1)} %get-tuple-element.654, ...), kind=kLoop, calls=%fused_computation.593 | loop fusion | flops 5447680 | bytes 9363304 | tf_op jit(solution)/shard_map/convert_element_type | solution.py:193
  171.5 6.1 %while.56 = (s32[]{:T(128)}, f32[4,512]{1,0:T(4,128)S(1)}, s32[4,512]{1,0:T(4,128)S(1)}, f32[4,3,512]{2,1,0:T(4,128)S(1)}, bf16[35,2432]{1,0:T(8,128)(2,1)S(1)}, /*index=5*/s32[]{:T(128)}, s32[]{:T(128)}, s32[]{}, s32[]{}) while((s32[]{:T(128)}, f32[4,512]{1,0:T(4,128)S(1)}, s32[4,512]{1,0:T(4,128)S(1)}, f32[4,3,512]{2,1,0:T(4,128)S(1)}, ...), condition=%wide.region_8.9_spmd, body=%wide.region_6.8_spmd.sunk | while | flops 90826240 | bytes 5958033 | solution.py:104
  177.6 3.0 %while.57 = (s32[]{:T(128)}, f32[2,512]{1,0:T(2,128)S(1)}, s32[2,512]{1,0:T(2,128)S(1)}, f32[2,3,512]{2,1,0:T(4,128)S(1)}, bf16[35,2432]{1,0:T(8,128)(2,1)S(1)}, /*index=5*/s32[]{:T(128)}, s32[]{:T(128)}, s32[]{}, s32[]{}) while((s32[]{:T(128)}, f32[2,512]{1,0:T(2,128)S(1)}, s32[2,512]{1,0:T(2,128)S(1)}, f32[2,3,512]{2,1,0:T(4,128)S(1)}, ...), condition=%wide.region_11.12_spmd, body=%wide.region_9.11_spmd.sunk | while | flops 90826240 | bytes 5958033 | solution.py:104
  (249 shorter events, 34.2 us)
Async XLA Ops:
  0.6 16.9 %copy-start = (f32[3,13]{1,0:T(4,128)S(1)}, f32[3,13]{1,0:T(4,128)}, u32[]{:S(2)}) copy-start(f32[3,13]{1,0:T(4,128)} %param.31) | copy-start | bytes 472
  0.6 18.4 %copy-start.3 = (s32[2048]{0:T(1024)S(1)}, s32[2048]{0:T(1024)}, u32[]{:S(2)}) copy-start(s32[2048]{0:T(1024)} %param.24) | copy-start | bytes 24580
  0.7 19.0 %copy-start.4 = (f32[2048]{0:T(1024)S(1)}, f32[2048]{0:T(1024)}, u32[]{:S(2)}) copy-start(f32[2048]{0:T(1024)} %param.22) | copy-start | bytes 24580
  0.7 19.1 %copy-start.2 = (f32[3,2048]{1,0:T(4,128)S(1)}, f32[3,2048]{1,0:T(4,128)}, u32[]{:S(2)}) copy-start(f32[3,2048]{1,0:T(4,128)} %param.23) | copy-start | bytes 73732
  5.9 24.9 %all-to-all-start = ((f32[5,128,8]{2,0,1:T(8,128)}), f32[5,128,8]{2,0,1:T(8,128)}, u32[]{:S(2)}, u32[]{:S(2)}) async-start(f32[5,128,8]{2,0,1:T(8,128)} %copy.17), calls=%async_computation | async-start | bytes 1048576 | tf_op jit(solution)/shard_map/all_to_all | solution.py:169
  19.7 9.6 %copy-start.1 = (f32[3,13]{1,0:T(4,128)S(1)}, f32[3,13]{1,0:T(4,128)}, u32[]{:S(2)}) copy-start(f32[3,13]{1,0:T(4,128)} %param.30) | copy-start | bytes 472
  39.7 7.1 %collective-permute-start = (f32[3,19,128]{2,1,0:T(8,128)S(1)}, f32[3,19,128]{2,1,0:T(8,128)S(1)}, u32[]{:S(2)}, u32[]{:S(2)}) collective-permute-start(f32[3,19,128]{2,1,0:T(8,128)S(1)} %slice.957), channel_id=1, source_target_pairs={{0,8},{8,16},{16,24},{24,32},{32,40},{40,48},{48,56},{56,64},{64,7... | collective-permute-start | bytes 87560 | tf_op jit(solution)/shard_map/ppermute | solution.py:14
  46.8 6.4 %collective-permute-start.1 = (f32[32,3,128]{2,1,0:T(4,128)S(1)}, f32[32,3,128]{2,1,0:T(4,128)S(1)}, u32[]{:S(2)}, u32[]{:S(2)}) collective-permute-start(f32[32,3,128]{2,1,0:T(4,128)S(1)} %slice.1158), channel_id=1, source_target_pairs={{0,1},{1,2},{2,3},{3,4},{4,5},{5,6},{6,7},{7,0},{8,9},{9,10},{10,1... | collective-permute-start | bytes 147464 | tf_op jit(solution)/shard_map/ppermute | solution.py:14
  78.6 5.6 %collective-permute-start.7 = (f32[8,8,64]{2,1,0:T(8,128)S(1)}, f32[8,8,64]{2,1,0:T(8,128)S(1)}, u32[]{:S(2)}, u32[]{:S(2)}) collective-permute-start(f32[8,8,64]{2,1,0:T(8,128)S(1)} %get-tuple-element.704), channel_id=1, source_target_pairs={{8,0},{16,8},{24,16},{32,24},{40,32},{48,40},{56,48},{64,56},{72,6... | collective-permute-start | bytes 49160 | tf_op jit(solution)/shard_map/ppermute | solution.py:25
  78.7 7.0 %collective-permute-start.6 = (f32[8,8,64]{2,1,0:T(8,128)S(1)}, f32[8,8,64]{2,1,0:T(8,128)S(1)}, u32[]{:S(2)}, u32[]{:S(2)}) collective-permute-start(f32[8,8,64]{2,1,0:T(8,128)S(1)} %get-tuple-element.703), channel_id=1, source_target_pairs={{0,8},{8,16},{16,24},{24,32},{32,40},{40,48},{48,56},{56,64},{64,7... | collective-permute-start | bytes 49160 | tf_op jit(solution)/shard_map/ppermute | solution.py:24
  79.2 8.7 %collective-permute-start.3 = (f32[9,16,128]{2,1,0:T(8,128)S(1)}, f32[9,16,128]{2,1,0:T(8,128)S(1)}, u32[]{:S(2)}, u32[]{:S(2)}) collective-permute-start(f32[9,16,128]{2,1,0:T(8,128)S(1)} %get-tuple-element.678), channel_id=1, source_target_pairs={{8,0},{16,8},{24,16},{32,24},{40,32},{48,40},{56,48},{64,56},{72,6... | collective-permute-start | bytes 221192 | tf_op jit(solution)/shard_map/ppermute | solution.py:25
  84.2 7.5 %collective-permute-start.2 = (f32[9,16,128]{2,1,0:T(8,128)S(1)}, f32[9,16,128]{2,1,0:T(8,128)S(1)}, u32[]{:S(2)}, u32[]{:S(2)}) collective-permute-start(f32[9,16,128]{2,1,0:T(8,128)S(1)} %get-tuple-element.677), channel_id=1, source_target_pairs={{0,8},{8,16},{16,24},{24,32},{32,40},{40,48},{48,56},{56,64},{64,7... | collective-permute-start | bytes 221192 | tf_op jit(solution)/shard_map/ppermute | solution.py:24
  85.8 8.1 %collective-permute-start.9 = (f32[32,8,64]{2,1,0:T(8,128)S(1)}, f32[32,8,64]{2,1,0:T(8,128)S(1)}, u32[]{:S(2)}, u32[]{:S(2)}) collective-permute-start(f32[32,8,64]{2,1,0:T(8,128)S(1)} %pad_maximum_fusion.3), channel_id=1, source_target_pairs={{1,0},{2,1},{3,2},{4,3},{5,4},{6,5},{7,6},{0,7},{9,8},{10,9},{11,1... | collective-permute-start | bytes 196616 | tf_op jit(solution)/shard_map/ppermute | solution.py:25
  86.8 8.5 %collective-permute-start.8 = (f32[32,8,64]{2,1,0:T(8,128)S(1)}, f32[32,8,64]{2,1,0:T(8,128)S(1)}, u32[]{:S(2)}, u32[]{:S(2)}) collective-permute-start(f32[32,8,64]{2,1,0:T(8,128)S(1)} %pad_maximum_fusion.3), channel_id=1, source_target_pairs={{0,1},{1,2},{2,3},{3,4},{4,5},{5,6},{6,7},{7,0},{8,9},{9,10},{10,1... | collective-permute-start | bytes 196616 | tf_op jit(solution)/shard_map/ppermute | solution.py:24
  91.8 40.0 %collective-permute-start.5 = (f32[50,9,128]{2,1,0:T(8,128)S(1)}, f32[50,9,128]{2,1,0:T(8,128)S(1)}, u32[]{:S(2)}, u32[]{:S(2)}) collective-permute-start(f32[50,9,128]{2,1,0:T(8,128)S(1)} %get-tuple-element.674), channel_id=1, source_target_pairs={{1,0},{2,1},{3,2},{4,3},{5,4},{6,5},{7,6},{0,7},{9,8},{10,9},{11,1... | collective-permute-start | bytes 691208 | tf_op jit(solution)/shard_map/ppermute | solution.py:25
  92.7 39.1 %collective-permute-start.4 = (f32[50,9,128]{2,1,0:T(8,128)S(1)}, f32[50,9,128]{2,1,0:T(8,128)}, u32[]{:S(2)}, u32[]{:S(2)}) collective-permute-start(f32[50,9,128]{2,1,0:T(8,128)S(1)} %get-tuple-element.673), channel_id=1, source_target_pairs={{0,1},{1,2},{2,3},{3,4},{4,5},{5,6},{6,7},{7,0},{8,9},{9,10},{10,1... | collective-permute-start | bytes 691208 | tf_op jit(solution)/shard_map/ppermute | solution.py:24
where the time goes:
time: 184 us; the launch traced here: 183 us
  other arithmetic  92.7 us (50%)
  local copies, waits for them, and re-layouts  33.2 us (18%)
  starting transfers between devices  21.9 us (12%)
  waiting for transfers between devices  17 us (9%)
  matrix products  14.7 us (8%)
  between operations  1.84 us (1%)
    add x4, other arithmetic, along(): summed + filter_taps[tap_index] * lax.slice_in_dim(field, offset + tap_in...  34 us
    convert_element_type x1, other arithmetic, on_device(): half_grid = field_ext.astype(jnp.bfloat16).reshape(CX + 3, (CY + 3) * NZ)  18.6 us
    reshape x1, local copies, waits for them, and re-layouts, coarsen(): field.reshape(size_a // 2, 2, size_b // 2, 2, size_c // 2, 2)  18.1 us
    add x1, other arithmetic, beside_all(): summed + filter_taps[tap_index] * jnp.roll(field, half_width - tap_index,...  17 us
    all_to_all x1, starting transfers between devices, on_device(): lax.all_to_all(packed.reshape(5, devices, slots), ('gx', 'gy'), split_axi...  11.7 us
    ppermute x2, waiting for transfers between devices, from_behind(): return lax.ppermute(value, axis, pairs)  9.57 us
    dot_general x6, matrix products, advance(): lax.dot_general(x_charge, yz_weights, (((0,), (0,)), ((), ())), preferred...  8.92 us
    convert_element_type x12, other arithmetic, factors(): (y_weights[:, :, None] * z_weights[:, None, :]).astype(jnp.bfloat16)  7.11 us
  transfers between devices with their start and end apart: 11, of which 6 were waited for; matrix products, arithmetic and copies ran while one was open for 28% of the time, Pallas kernels for 0%

commit v1 on v0

--- a/solution.py
+++ b/solution.py
@@ -166,9 +166,11 @@
         [mov_charge[None, :], mov_frac, (mov_cell.astype(jnp.float32) + 1.0)[None, :]], 0
     )
     packed = jnp.dot(payload, placing, precision=lax.Precision.HIGHEST)
-    arrived = lax.all_to_all(
-        packed.reshape(5, devices, slots), ("gx", "gy"), split_axis=1, concat_axis=1, tiled=True
-    )
+    array = packed.reshape(5, devices, slots)
+    count_2 = lax.axis_size(("gx", "gy"))
+    parts = jnp.stack(jnp.split(array, count_2, axis=1), axis=0)
+    parts = lax.all_to_all(parts, ("gx", "gy"), split_axis=0, concat_axis=0)
+    arrived = jnp.concatenate(parts, axis=1)
     arrived = arrived.reshape(5, devices * slots)
     live = jnp.arange(res_charge.shape[0], dtype=jnp.int32) < res_count[0]
     live_charge = jnp.where(live, res_charge, 0.0)

time: 184 us -> 185 us (level)
    another operation x1 -> x10, local copies, waits for them, and re-layouts: 0.02 us -> 2.05 us  [the longest x9 2.04 us: on_device(): parts = jnp.stack(jnp.split(array, count_2, axis=1), axis=0)]
  transfers between devices with their start and end apart: 11 -> 11, of which waited for: 6 -> 5; matrix products, arithmetic and copies ran while one was open for 28% -> 28% of each run, Pallas kernels for 0% -> 0%
where the time goes in v1:
time: 185 us; the launch traced here: 184 us
  other arithmetic  92.6 us (50%)
  local copies, waits for them, and re-layouts  34 us (18%)
  starting transfers between devices  23 us (12%)
  waiting for transfers between devices  16.2 us (9%)
  matrix products  14.7 us (8%)
  between operations  1.91 us (1%)
    add x4, other arithmetic, along(): summed + filter_taps[tap_index] * lax.slice_in_dim(field, offset + tap_in...  34.1 us
    convert_element_type x1, other arithmetic, on_device(): half_grid = field_ext.astype(jnp.bfloat16).reshape(CX + 3, (CY + 3) * NZ)  18.8 us
    reshape x1, local copies, waits for them, and re-layouts, coarsen(): field.reshape(size_a // 2, 2, size_b // 2, 2, size_c // 2, 2)  18.1 us
    add x1, other arithmetic, beside_all(): summed + filter_taps[tap_index] * jnp.roll(field, half_width - tap_index,...  17 us
    all_to_all x1, starting transfers between devices, on_device(): parts = lax.all_to_all(parts, ('gx', 'gy'), split_axis=0, concat_axis=0)  11.6 us
    ppermute x2, waiting for transfers between devices, from_behind(): return lax.ppermute(value, axis, pairs)  9.04 us
    dot_general x6, matrix products, advance(): lax.dot_general(x_charge, yz_weights, (((0,), (0,)), ((), ())), preferred...  8.92 us
    ppermute x4, starting transfers between devices, padded_2(): after = lax.ppermute(initial, axis, down)  8.63 us
  transfers between devices with their start and end apart: 11, of which 5 were waited for; matrix products, arithmetic and copies ran while one was open for 28% of the time, Pallas kernels for 0%

profile of v1, /device:TPU:0, one launch (start us, length us, event | category | flops | bytes accessed | tf_op | source)
XLA Modules:
  0.0 183.6 jit_solution(15289435947785960863)
XLA Ops:
  3.1 1.5 fusion.156
  5.9 1.1 copy.288
  6.9 11.6 %all-to-all-start = ((f32[128,5,1,8]{3,2,1,0:T(1,128)}), f32[128,5,1,8]{3,2,1,0:T(1,128)}, u32[]{:S(2)}, u32[]{:S(2)}) async-start(f32[128,5,1,8]{3,2,1,0:T(1,128)} %copy.288), calls=%async_computation | async-start | bytes 655360 | tf_op jit(solution)/shard_map/all_to_all | solution.py:172
  20.8 9.6 %while.58 = (s32[]{:T(128)}, f32[35,2432]{1,0:T(8,128)S(1)}, s32[4,512]{1,0:T(4,128)S(1)}, f32[4,3,512]{2,1,0:T(4,128)S(1)}, f32[4,512]{1,0:T(4,128)S(1)}, /*index=5*/s32[]{:T(128)}, s32[]{:T(128)}, s32[]{}, s32[]{}) while((s32[]{:T(128)}, f32[35,2432]{1,0:T(8,128)S(1)}, s32[4,512]{1,0:T(4,128)S(1)}, f32[4,3,512]{2,1,0:T(4,128)S(1)}, ...), condition=%wide.region_1.2_spmd.clone, body=%wide.region_0.0_spmd.clone.sunk | while | flops 90961152 | bytes 6397083 | solution.py:89
  21.7 1.5 convolution_add_fusion.4
  24.1 1.5 convolution_add_fusion.4
  26.5 1.5 convolution_add_fusion.4
  28.9 1.5 convolution_add_fusion.4
  31.1 1.1 convert_reduce_fusion
  34.6 4.8 %while.59 = (s32[]{:T(128)}, f32[35,2432]{1,0:T(8,128)S(1)}, s32[2,512]{1,0:T(2,128)S(1)}, f32[2,3,512]{2,1,0:T(4,128)S(1)}, f32[2,512]{1,0:T(2,128)S(1)}, /*index=5*/s32[]{:T(128)}, s32[]{:T(128)}, s32[]{}, s32[]{}) while((s32[]{:T(128)}, f32[35,2432]{1,0:T(8,128)S(1)}, s32[2,512]{1,0:T(2,128)S(1)}, f32[2,3,512]{2,1,0:T(4,128)S(1)}, ...), condition=%wide.region_4.5_spmd.clone, body=%wide.region_3.4_spmd.clone.sunk | while | flops 90961152 | bytes 6397083 | solution.py:89
  35.5 1.5 convolution_add_fusion.5
  37.9 1.5 convolution_add_fusion.5
  41.7 4.9 %collective-permute-done = f32[3,19,128]{2,1,0:T(8,128)S(1)} collective-permute-done((f32[3,19,128]{2,1,0:T(8,128)S(1)}, f32[3,19,128]{2,1,0:T(8,128)S(1)}, u32[]{:S(2)}, u32[]{:S(2)}) %collective-permute-start) | collective-permute-done | bytes 29216 | tf_op jit(solution)/shard_map/ppermute | solution.py:14
  46.6 1.1 collective-permute-start.1
  48.9 4.2 %collective-permute-done.1 = f32[32,3,128]{2,1,0:T(4,128)S(1)} collective-permute-done((f32[32,3,128]{2,1,0:T(4,128)S(1)}, f32[32,3,128]{2,1,0:T(4,128)S(1)}, u32[]{:S(2)}, u32[]{:S(2)}) %collective-permute-start.1) | collective-permute-done | bytes 49184 | tf_op jit(solution)/shard_map/ppermute | solution.py:14
  53.3 18.1 %reshape.3267 = f32[16,2,8,2,64,2]{5,4,3,2,1,0:T(8,128)} reshape(f32[32,16,128]{2,1,0:T(8,128)S(1)} %scatter-add.9) | data formatting | bytes 524288 | tf_op jit(solution)/shard_map/reshape | solution.py:135
  71.4 7.0 %reduce_sum.45 = f32[16,8,64]{2,1,0:T(8,128)S(1)} reduce(f32[16,2,8,2,64,2]{5,4,3,2,1,0:T(8,128)} %reshape.3267, f32[]{:T(128)} %constant.878.clone.1), dimensions={1,3,5}, to_apply=%region_5.6 | reduce | flops 57344 | bytes 294916 | tf_op jit(solution)/shard_map/reduce_sum | solution.py:135
  79.2 5.3 %collective-permute-start.3 = (f32[9,16,128]{2,1,0:T(8,128)S(1)}, f32[9,16,128]{2,1,0:T(8,128)S(1)}, u32[]{:S(2)}, u32[]{:S(2)}) collective-permute-start(f32[9,16,128]{2,1,0:T(8,128)S(1)} %get-tuple-element.826), channel_id=1, source_target_pairs={{8,0},{16,8},{24,16},{32,24},{40,32},{48,40},{56,48},{64,56},{72,6... | collective-permute-start | bytes 221192 | tf_op jit(solution)/shard_map/ppermute | solution.py:25
  84.5 1.5 collective-permute-done.6
  86.0 1.4 collective-permute-start.9
  88.1 3.9 %collective-permute-done.2 = f32[9,16,128]{2,1,0:T(8,128)S(1)} collective-permute-done((f32[9,16,128]{2,1,0:T(8,128)S(1)}, f32[9,16,128]{2,1,0:T(8,128)S(1)}, u32[]{:S(2)}, u32[]{:S(2)}) %collective-permute-start.2) | collective-permute-done | bytes 73760 | tf_op jit(solution)/shard_map/ppermute | solution.py:24
  92.1 1.3 collective-permute-start.5
  94.2 1.8 collective-permute-done.8
  96.0 8.3 %fusion.196 = f32[18,24,64]{2,1,0:T(8,128)S(1)} fusion(f32[32,24,64]{2,1,0:T(8,128)S(1)} %pad_maximum_fusion.2, f32[]{:T(128)} %bitcast.204, f32[]{:T(128)} %bitcast.203, f32[]{:T(128)} %bitcast.202, f32[]{:T(128)} %bitcast.201, f32[]{:T(128)} %bitcast.200, f32[]{:T(128)} %bitcast.199, f32[]{:T(128)} %bitcast.198, f32[]{:T(128)} %bitcast.197, f32[]{:T(128)} %bitcast.196, ...), kind=kLoop, calls=%fused_computation.501 | loop fusion | flops 691200 | bytes 1548340 | tf_op jit(solution)/shard_map/add | solution.py:112
  104.3 8.2 %fusion.208 = f32[18,10,64]{2,1,0:T(8,128)S(1)} fusion(f32[18,24,64]{2,1,0:T(8,128)S(1)} %fusion.196, f32[]{:T(128)} %bitcast.216, f32[]{:T(128)} %bitcast.215, f32[]{:T(128)} %bitcast.214, f32[]{:T(128)} %bitcast.213, f32[]{:T(128)} %bitcast.212, f32[]{:T(128)} %bitcast.211, f32[]{:T(128)} %bitcast.210, f32[]{:T(128)} %bitcast.209, f32[]{:T(128)} %bitcast.208, ...), kind=kLoop, calls=%fused_computation.526 | loop fusion | flops 288000 | bytes 645172 | tf_op jit(solution)/shard_map/add | solution.py:112
  113.8 17.0 %fusion.231 = f32[18,10,64]{2,1,0:T(8,128)S(1)} fusion(f32[18,10,58]{2,1,0:T(8,128)S(1)} %get-tuple-element.828, f32[18,10,6]{2,1,0:T(8,128)S(1)} %get-tuple-element.830, f32[18,10,59]{2,1,0:T(8,128)S(1)} %get-tuple-element.832, f32[18,10,5]{2,1,0:T(8,128)S(1)} %get-tuple-element.834, f32[18,10,60]{2,1,0:T(8,128)S(1)} %get-tuple-element.836, ...), kind=kLoop, calls=%fused_computation.562 | loop fusion | flops 714240 | bytes 1198184 | tf_op jit(solution)/shard_map/add | solution.py:122
  132.5 1.1 pad_maximum_fusion
  133.6 8.8 %fusion.159 = f32[35,34,128]{2,1,0:T(8,128)S(1)} fusion(f32[50,34,128]{2,1,0:T(8,128)S(1)} %pad_maximum_fusion, f32[]{:T(128)} %bitcast.165, f32[]{:T(128)} %bitcast.164, f32[]{:T(128)} %bitcast.163, f32[]{:T(128)} %bitcast.162, f32[]{:T(128)} %bitcast.161, f32[]{:T(128)} %bitcast.160, f32[]{:T(128)} %bitcast.159, f32[]{:T(128)} %bitcast.158, f32[]{:T(128)} %bitcast.157, ...), kind=kLoop, calls=%fused_computation.422 | loop fusion | flops 3808000 | bytes 8529972 | tf_op jit(solution)/shard_map/add | solution.py:112
  142.4 8.9 %fusion.171 = f32[35,19,128]{2,1,0:T(8,128)S(1)} fusion(f32[35,34,128]{2,1,0:T(8,128)S(1)} %fusion.159, f32[]{:T(128)} %bitcast.177, f32[]{:T(128)} %bitcast.176, f32[]{:T(128)} %bitcast.175, f32[]{:T(128)} %bitcast.174, f32[]{:T(128)} %bitcast.173, f32[]{:T(128)} %bitcast.172, f32[]{:T(128)} %bitcast.171, f32[]{:T(128)} %bitcast.170, f32[]{:T(128)} %bitcast.169, ...), kind=kLoop, calls=%fused_computation.447 | loop fusion | flops 2128000 | bytes 4766772 | tf_op jit(solution)/shard_map/add | solution.py:112
  153.7 18.8 %fusion.241 = (bf16[35,19,128]{2,1,0:T(8,128)(2,1)S(1)}, f32[35,19,128]{2,1,0:T(8,128)S(1)}) fusion(f32[35,19,128]{2,1,0:T(8,128)S(1)} %copy.295, f32[35,19,6]{2,1,0:T(8,128)S(1)} %get-tuple-element.670, f32[35,19,122]{2,1,0:T(8,128)S(1)} %get-tuple-element.672, f32[]{:T(128)} %bitcast.189, f32[35,19,5]{2,1,0:T(8,128)S(1)} %get-tuple-element.674, ...), kind=kLoop, calls=%fused_computation.721 | loop fusion | flops 5447680 | bytes 9363304 | tf_op jit(solution)/shard_map/convert_element_type | solution.py:195
  172.5 6.1 %while.56 = (s32[]{:T(128)}, f32[4,512]{1,0:T(4,128)S(1)}, s32[4,512]{1,0:T(4,128)S(1)}, f32[4,3,512]{2,1,0:T(4,128)S(1)}, bf16[35,2432]{1,0:T(8,128)(2,1)S(1)}, /*index=5*/s32[]{:T(128)}, s32[]{:T(128)}, s32[]{}, s32[]{}) while((s32[]{:T(128)}, f32[4,512]{1,0:T(4,128)S(1)}, s32[4,512]{1,0:T(4,128)S(1)}, f32[4,3,512]{2,1,0:T(4,128)S(1)}, ...), condition=%wide.region_8.9_spmd, body=%wide.region_6.8_spmd.sunk | while | flops 90826240 | bytes 5958033 | solution.py:104
  178.6 3.0 %while.57 = (s32[]{:T(128)}, f32[2,512]{1,0:T(2,128)S(1)}, s32[2,512]{1,0:T(2,128)S(1)}, f32[2,3,512]{2,1,0:T(4,128)S(1)}, bf16[35,2432]{1,0:T(8,128)(2,1)S(1)}, /*index=5*/s32[]{:T(128)}, s32[]{:T(128)}, s32[]{}, s32[]{}) while((s32[]{:T(128)}, f32[2,512]{1,0:T(2,128)S(1)}, s32[2,512]{1,0:T(2,128)S(1)}, f32[2,3,512]{2,1,0:T(4,128)S(1)}, ...), condition=%wide.region_11.12_spmd, body=%wide.region_9.11_spmd.sunk | while | flops 90826240 | bytes 5958033 | solution.py:104
  (257 shorter events, 34.9 us)
Async XLA Ops:
  0.6 17.9 %copy-start = (f32[3,13]{1,0:T(4,128)S(1)}, f32[3,13]{1,0:T(4,128)}, u32[]{:S(2)}) copy-start(f32[3,13]{1,0:T(4,128)} %param.31) | copy-start | bytes 472
  0.6 19.4 %copy-start.3 = (s32[2048]{0:T(1024)S(1)}, s32[2048]{0:T(1024)}, u32[]{:S(2)}) copy-start(s32[2048]{0:T(1024)} %param.24) | copy-start | bytes 24580
  0.7 20.1 %copy-start.4 = (f32[2048]{0:T(1024)S(1)}, f32[2048]{0:T(1024)}, u32[]{:S(2)}) copy-start(f32[2048]{0:T(1024)} %param.22) | copy-start | bytes 24580
  0.7 20.1 %copy-start.2 = (f32[3,2048]{1,0:T(4,128)S(1)}, f32[3,2048]{1,0:T(4,128)}, u32[]{:S(2)}) copy-start(f32[3,2048]{1,0:T(4,128)} %param.23) | copy-start | bytes 73732
  6.9 24.2 %all-to-all-start = ((f32[128,5,1,8]{3,2,1,0:T(1,128)}), f32[128,5,1,8]{3,2,1,0:T(1,128)}, u32[]{:S(2)}, u32[]{:S(2)}) async-start(f32[128,5,1,8]{3,2,1,0:T(1,128)} %copy.288), calls=%async_computation | async-start | bytes 655360 | tf_op jit(solution)/shard_map/all_to_all | solution.py:172
  20.8 9.6 %copy-start.1 = (f32[3,13]{1,0:T(4,128)S(1)}, f32[3,13]{1,0:T(4,128)}, u32[]{:S(2)}) copy-start(f32[3,13]{1,0:T(4,128)} %param.30) | copy-start | bytes 472
  39.5 7.1 %collective-permute-start = (f32[3,19,128]{2,1,0:T(8,128)S(1)}, f32[3,19,128]{2,1,0:T(8,128)S(1)}, u32[]{:S(2)}, u32[]{:S(2)}) collective-permute-start(f32[3,19,128]{2,1,0:T(8,128)S(1)} %slice.957), channel_id=1, source_target_pairs={{0,8},{8,16},{16,24},{24,32},{32,40},{40,48},{48,56},{56,64},{64,7... | collective-permute-start | bytes 87560 | tf_op jit(solution)/shard_map/ppermute | solution.py:14
  46.6 6.4 %collective-permute-start.1 = (f32[32,3,128]{2,1,0:T(4,128)S(1)}, f32[32,3,128]{2,1,0:T(4,128)S(1)}, u32[]{:S(2)}, u32[]{:S(2)}) collective-permute-start(f32[32,3,128]{2,1,0:T(4,128)S(1)} %slice.1158), channel_id=1, source_target_pairs={{0,1},{1,2},{2,3},{3,4},{4,5},{5,6},{6,7},{7,0},{8,9},{9,10},{10,1... | collective-permute-start | bytes 147464 | tf_op jit(solution)/shard_map/ppermute | solution.py:14
  78.4 6.1 %collective-permute-start.7 = (f32[8,8,64]{2,1,0:T(8,128)S(1)}, f32[8,8,64]{2,1,0:T(8,128)S(1)}, u32[]{:S(2)}, u32[]{:S(2)}) collective-permute-start(f32[8,8,64]{2,1,0:T(8,128)S(1)} %get-tuple-element.852), channel_id=1, source_target_pairs={{8,0},{16,8},{24,16},{32,24},{40,32},{48,40},{56,48},{64,56},{72,6... | collective-permute-start | bytes 49160 | tf_op jit(solution)/shard_map/ppermute | solution.py:25
  79.0 7.0 %collective-permute-start.6 = (f32[8,8,64]{2,1,0:T(8,128)S(1)}, f32[8,8,64]{2,1,0:T(8,128)S(1)}, u32[]{:S(2)}, u32[]{:S(2)}) collective-permute-start(f32[8,8,64]{2,1,0:T(8,128)S(1)} %get-tuple-element.851), channel_id=1, source_target_pairs={{0,8},{8,16},{16,24},{24,32},{32,40},{40,48},{48,56},{56,64},{64,7... | collective-permute-start | bytes 49160 | tf_op jit(solution)/shard_map/ppermute | solution.py:24
  79.2 8.9 %collective-permute-start.3 = (f32[9,16,128]{2,1,0:T(8,128)S(1)}, f32[9,16,128]{2,1,0:T(8,128)S(1)}, u32[]{:S(2)}, u32[]{:S(2)}) collective-permute-start(f32[9,16,128]{2,1,0:T(8,128)S(1)} %get-tuple-element.826), channel_id=1, source_target_pairs={{8,0},{16,8},{24,16},{32,24},{40,32},{48,40},{56,48},{64,56},{72,6... | collective-permute-start | bytes 221192 | tf_op jit(solution)/shard_map/ppermute | solution.py:25
  84.5 7.5 %collective-permute-start.2 = (f32[9,16,128]{2,1,0:T(8,128)S(1)}, f32[9,16,128]{2,1,0:T(8,128)S(1)}, u32[]{:S(2)}, u32[]{:S(2)}) collective-permute-start(f32[9,16,128]{2,1,0:T(8,128)S(1)} %get-tuple-element.825), channel_id=1, source_target_pairs={{0,8},{8,16},{16,24},{24,32},{32,40},{40,48},{48,56},{56,64},{64,7... | collective-permute-start | bytes 221192 | tf_op jit(solution)/shard_map/ppermute | solution.py:24
  86.0 8.2 %collective-permute-start.9 = (f32[32,8,64]{2,1,0:T(8,128)S(1)}, f32[32,8,64]{2,1,0:T(8,128)S(1)}, u32[]{:S(2)}, u32[]{:S(2)}) collective-permute-start(f32[32,8,64]{2,1,0:T(8,128)S(1)} %pad_maximum_fusion.3), channel_id=1, source_target_pairs={{1,0},{2,1},{3,2},{4,3},{5,4},{6,5},{7,6},{0,7},{9,8},{10,9},{11,1... | collective-permute-start | bytes 196616 | tf_op jit(solution)/shard_map/ppermute | solution.py:25
  87.4 8.5 %collective-permute-start.8 = (f32[32,8,64]{2,1,0:T(8,128)S(1)}, f32[32,8,64]{2,1,0:T(8,128)S(1)}, u32[]{:S(2)}, u32[]{:S(2)}) collective-permute-start(f32[32,8,64]{2,1,0:T(8,128)S(1)} %pad_maximum_fusion.3), channel_id=1, source_target_pairs={{0,1},{1,2},{2,3},{3,4},{4,5},{5,6},{6,7},{7,0},{8,9},{9,10},{10,1... | collective-permute-start | bytes 196616 | tf_op jit(solution)/shard_map/ppermute | solution.py:24
  92.1 40.4 %collective-permute-start.5 = (f32[50,9,128]{2,1,0:T(8,128)S(1)}, f32[50,9,128]{2,1,0:T(8,128)S(1)}, u32[]{:S(2)}, u32[]{:S(2)}) collective-permute-start(f32[50,9,128]{2,1,0:T(8,128)S(1)} %get-tuple-element.694), channel_id=1, source_target_pairs={{1,0},{2,1},{3,2},{4,3},{5,4},{6,5},{7,6},{0,7},{9,8},{10,9},{11,1... | collective-permute-start | bytes 691208 | tf_op jit(solution)/shard_map/ppermute | solution.py:25
  93.4 39.1 %collective-permute-start.4 = (f32[50,9,128]{2,1,0:T(8,128)S(1)}, f32[50,9,128]{2,1,0:T(8,128)}, u32[]{:S(2)}, u32[]{:S(2)}) collective-permute-start(f32[50,9,128]{2,1,0:T(8,128)S(1)} %get-tuple-element.693), channel_id=1, source_target_pairs={{0,1},{1,2},{2,3},{3,4},{4,5},{5,6},{6,7},{7,0},{8,9},{9,10},{10,1... | collective-permute-start | bytes 691208 | tf_op jit(solution)/shard_map/ppermute | solution.py:24
